TPU v7x, 32 devices: a whole 2x2x4 slice. The times are simulated.
32 devices in a mesh: dp: 8 (over y, x, core), tensor: 4 (over z).
Axes of the slice: x: 2, y: 2, z: 4, core: 2. Of those that a mesh axis runs over, the one named last changes fastest.
Arguments:
- teacher_hidden: bfloat16 [1024, 4096], P('dp'), may hold values from -6 to 6
- student_hidden: bfloat16 [1024, 2048], P('dp'), may hold values from -6 to 6
- target_ids: int32 [1024], P('dp'), may hold values from 0 to 64127
- teacher_head: bfloat16 [4096, 65536], P(None, ('dp', 'tensor')), may hold values from -1 to 1
- student_head: bfloat16 [2048, 65536], P(None, ('dp', 'tensor')), may hold values from -1 to 1
Outputs:
- head_grad: float32 [2048, 65536], P(None, ('dp', 'tensor'))
- input_grad: float32 [1024, 2048], P('dp', 'tensor')
All inputs are finite; a program needn't handle non-finite values.
Results may differ from a plain program's by a relative error of at most 0.0065.
Values may be sent and summed in bfloat16 or wider, within the bound.
A program may use at most 128 MiB of HBM per device.

v0:
```python
import jax
import jax.numpy as jnp
from jax import lax
from jax.sharding import PartitionSpec as P

VOCAB = 64128


def body(teacher_hidden, student_hidden, target_ids, teacher_head, student_head):
    width_cols = teacher_head.shape[1]
    first_col = (
        lax.axis_index("dp") * lax.axis_size("tensor") + lax.axis_index("tensor")
    ) * width_cols
    columns = first_col + lax.iota(jnp.int32, width_cols)
    is_real = (columns < VOCAB)[None, :]
    teacher_logits = jnp.dot(
        lax.all_gather(teacher_hidden, "dp", axis=0, tiled=True),
        teacher_head,
        preferred_element_type=jnp.float32,
    )
    teacher_logits = jnp.where(is_real, teacher_logits, jnp.float32(-1e30))
    student_rows, all_targets = (
        lax.all_gather(student_hidden, "dp", axis=0, tiled=True),
        lax.all_gather(target_ids, "dp", axis=0, tiled=True),
    )
    student_logits = jnp.where(
        is_real,
        jnp.dot(student_rows, student_head, preferred_element_type=jnp.float32),
        jnp.float32(-1e30),
    )
    teacher_peak, student_peak = lax.pmax(
        (jnp.max(teacher_logits, axis=1), jnp.max(student_logits, axis=1)), ("dp", "tensor")
    )
    teacher_expo = jnp.exp(teacher_logits - teacher_peak[:, None])
    student_expo = jnp.exp(student_logits - student_peak[:, None])
    teacher_total, student_total = lax.psum(
        (jnp.sum(teacher_expo, axis=1), jnp.sum(student_expo, axis=1)), ("dp", "tensor")
    )
    teacher_probs = teacher_expo / teacher_total[:, None]
    student_probs = student_expo / student_total[:, None]
    onehot = (all_targets[:, None] == columns[None, :]).astype(jnp.float32)
    logit_grad = (2.0 * student_probs - teacher_probs - onehot).astype(jnp.bfloat16)
    head_grad = lax.dot_general(
        student_rows, logit_grad, (((0,), (0,)), ((), ())), preferred_element_type=jnp.float32
    )
    own_rows = lax.psum_scatter(
        lax.dot_general(
            logit_grad, student_head, (((1,), (1,)), ((), ())), preferred_element_type=jnp.float32
        ),
        "dp",
        scatter_dimension=0,
        tiled=True,
    )
    input_grad = lax.psum_scatter(own_rows, "tensor", scatter_dimension=1, tiled=True)
    return (head_grad, input_grad)


def solution(mesh):
    placed = (
        P("dp", None),
        P("dp", None),
        P("dp"),
        P(None, ("dp", "tensor")),
        P(None, ("dp", "tensor")),
    )
    return jax.shard_map(
        body,
        mesh=mesh,
        in_specs=placed,
        out_specs=(P(None, ("dp", "tensor")), P("dp", "tensor")),
        check_vma=False,
    )
```

profile of v0, /device:TPU:0, one launch (start us, length us, event | category | flops | bytes accessed | tf_op | source)
XLA Modules:
  0.0 351.4 jit_solution(1641235967358725862)
XLA Ops:
  7.2 0.0 all-gather.4.cloned.1.call-start
  7.2 0.7 all-gather.4.cloned.1.call-update
  7.9 0.0 all-gather.6.cloned.1.call-start
  7.9 0.7 all-gather.6.cloned.1.call-update
  8.6 0.0 reduce-scatter.3.cloned.1.call-start
  8.7 10.4 %all-gather = s32[8,1,128]{2,1,0:T(1,128)S(1)} all-gather(s32[1,1,128]{2,1,0:T(1,128)} %bitcast.13), channel_id=1, replica_groups=mesh['dp'=8,'tensor'=4] {'dp'}, dimensions={0}, use_global_device_ids=true | all-gather | bytes 4608 | tf_op jit(solution)/shard_map/all_gather | solution.py:24
  19.1 30.1 %all-gather.4.cloned.1.call-done = bf16[1024,2048]{1,0:T(8,128)(2,1)} async-done(((bf16[128,2048]{1,0:T(8,128)(2,1)}), bf16[1024,2048]{1,0:T(8,128)(2,1)}) %all-gather.4.cloned.1.call-update) | async-done | bytes 4194320 | tf_op jit(solution)/shard_map/all_gather | solution.py:23
  49.2 14.5 %select_reduce_fusion.1 = (f32[1024]{0:T(1024)S(1)}, f32[1024,2048]{1,0:T(8,128)}) fusion(pred[2048]{0:T(1024)(128)(4,1)S(1)} %broadcast_compare_fusion, bf16[1024,2048]{1,0:T(8,128)(2,1)} %all-gather.4.cloned.1.call-done, bf16[2048,2048]{1,0:T(8,128)(2,1)} %param.9), kind=kOutput, calls=%fused_computation.5 | convolution fusion | flops 8594127872 | bytes 20977664 | tf_op jit(solution)/shard_map/dot_general | solution.py:28
  63.7 40.1 %pmax.14 = f32[1024]{0:T(1024)S(1)} all-reduce(f32[1024]{0:T(1024)S(1)} %get-tuple-element.10), channel_id=1, replica_groups=mesh['dp'=8,'tensor'=4] {'dp','tensor'}, use_global_device_ids=true, to_apply=%region_1.2 | all-reduce | flops 1024 | bytes 8192 | tf_op jit(solution)/shard_map/pmax | solution.py:31
  103.8 2.8 all-gather.6.cloned.1.call-done
  106.6 25.4 %fusion = (f32[1024]{0:T(1024)S(1)}, f32[1024]{0:T(1024)S(1)}, f32[1024,2048]{1,0:T(8,128)}) fusion(f32[1024,2048]{1,0:T(8,128)} %get-tuple-element.11, f32[1024]{0:T(1024)S(1)} %pmax.14, pred[2048]{0:T(1024)(128)(4,1)S(1)} %broadcast_compare_fusion, bf16[1024,4096]{1,0:T(8,128)(2,1)} %all-gather.6.cloned.1.call-done, bf16[4096,2048]{1,0:T(8,128)(2,1)} %param.8), kind=kOutput, calls=%fused_computation.6 | convolution fusion | flops 17190354944 | bytes 41957376 | tf_op jit(solution)/shard_map/dot_general | solution.py:16
  132.0 39.3 %pmax.15 = f32[1024]{0:T(1024)S(1)} all-reduce(f32[1024]{0:T(1024)S(1)} %get-tuple-element.7), channel_id=1, replica_groups=mesh['dp'=8,'tensor'=4] {'dp','tensor'}, use_global_device_ids=true, to_apply=%region_5.6 | all-reduce | flops 1024 | bytes 8192 | tf_op jit(solution)/shard_map/pmax | solution.py:31
  171.2 4.4 %fusion.1 = f32[1024]{0:T(1024)S(1)} fusion(f32[1024,2048]{1,0:T(8,128)} %get-tuple-element.12, f32[1024]{0:T(1024)S(1)} %pmax.15, pred[2048]{0:T(1024)(128)(4,1)S(1)} %broadcast_compare_fusion), kind=kLoop, calls=%fused_computation.7 | loop fusion | flops 6290432 | bytes 8398848 | tf_op jit(solution)/shard_map/reduce_sum | solution.py:37
  175.6 41.2 %all-reduce = (f32[1024]{0:T(1024)S(1)}, f32[1024]{0:T(1024)S(1)}) all-reduce(f32[1024]{0:T(1024)S(1)} %fusion.1, f32[1024]{0:T(1024)S(1)} %get-tuple-element.6), channel_id=1, replica_groups=mesh['dp'=8,'tensor'=4] {'dp','tensor'}, use_global_device_ids=true, to_apply=%region_7.8 | all-reduce | flops 2048 | bytes 16384 | tf_op jit(solution)/shard_map/psum | solution.py:36
  216.9 8.5 %subtract_convert_fusion = bf16[1024,2048]{1,0:T(8,128)(2,1)S(1)} fusion(f32[1024,2048]{1,0:T(8,128)} %get-tuple-element.11, f32[1024,2048]{1,0:T(8,128)} %get-tuple-element.12, s32[2048]{0:T(1024)S(1)} %iota_add_fusion, f32[1024]{0:T(1024)S(1)} %get-tuple-element.8, f32[1024]{0:T(1024)S(1)} %pmax.15, f32[1024]{0:T(1024)S(1)} %get-tuple-element.9, ...), kind=kLoop, calls=%fused_computation.1 | loop fusion | flops 25165824 | bytes 21002240 | tf_op jit(solution)/shard_map/convert_element_type | solution.py:42
  225.3 0.0 copy-start
  225.3 2.0 copy-done
  227.3 13.3 %fusion.2 = f32[1024,2048]{1,0:T(8,128)} fusion(bf16[1024,2048]{1,0:T(8,128)(2,1)S(1)} %subtract_convert_fusion, bf16[2048,2048]{1,0:T(8,128)(2,1)} %param.9), kind=kOutput, calls=%fused_computation.10 | convolution fusion | flops 8589934592 | bytes 20971520 | tf_op jit(solution)/shard_map/dot_general | solution.py:47
  240.6 0.0 reduce-scatter.3.cloned.1.call-update
  240.6 0.0 reduce-scatter.5.cloned.1.call-start
  240.6 71.4 %reduce-scatter.3.cloned.1.call-done = f32[128,2048]{1,0:T(8,128)} async-done(((f32[1024,2048]{1,0:T(8,128)}), f32[128,2048]{1,0:T(8,128)}) %reduce-scatter.3.cloned.1.call-update) | async-done | bytes 1048592 | tf_op jit(solution)/shard_map/reduce_scatter | solution.py:46
  312.0 0.0 reduce-scatter.5.cloned.1.call-update
  312.0 15.2 %convolution_bitcast_fusion = f32[2048,2048]{0,1:T(8,128)} fusion(bf16[1024,2048]{1,0:T(8,128)(2,1)} %copy-done, bf16[1024,2048]{1,0:T(8,128)(2,1)} %all-gather.4.cloned.1.call-done), kind=kOutput, calls=%fused_computation | convolution fusion | flops 8589934592 | bytes 25165824 | tf_op jit(solution)/shard_map/dot_general | solution.py:43
  327.2 17.6 %copy.8 = f32[2048,2048]{1,0:T(8,128)} copy(f32[2048,2048]{0,1:T(8,128)} %convolution_bitcast_fusion) | data formatting | bytes 33554432
  344.9 0.0 reduce-scatter.5.cloned.1.call-done
  (2 shorter events, 0.0 us)
Async XLA Ops:
  7.2 42.0 %all-gather.4.cloned.1.call-start = ((), (), s32[]{:S(2)}) async-start(), calls=%async_computation.2 | async-start | bytes 4718592 | tf_op jit(solution)/shard_map/all_gather | solution.py:23
  7.9 98.7 %all-gather.6.cloned.1.call-start = ((), (), s32[]{:S(2)}) async-start(), calls=%async_computation.3 | async-start | bytes 9437184 | tf_op jit(solution)/shard_map/all_gather | solution.py:17
  8.6 303.4 %reduce-scatter.3.cloned.1.call-start = ((), (), s32[]{:S(2)}) async-start(), calls=%async_computation.4 | async-start | bytes 9437184 | tf_op jit(solution)/shard_map/reduce_scatter | solution.py:46
  225.3 2.0 copy-start
  240.6 104.3 %reduce-scatter.5.cloned.1.call-start = ((), (), s32[]{:S(2)}) async-start(), calls=%async_computation.5 | async-start | bytes 1310720 | tf_op jit(solution)/shard_map/reduce_scatter | solution.py:54
Sparse Core Ops, SparseCore 0:
  9.9 39.2 all-gather.3
  51.1 55.4 all-gather.5
  240.7 71.2 reduce-scatter.2
  314.7 27.2 reduce-scatter.4
where the time goes:
time: 352 us; the launch traced here: 351 us
  blocking collectives  131 us (37%)
  waiting for transfers between devices  106 us (30%)
  matrix products  68.4 us (19%)
  local copies, waits for them, and re-layouts  19.6 us (6%)
  between operations  13.8 us (4%)
  other arithmetic  12.8 us (4%)
    pmax x2, blocking collectives, body(): lax.pmax((jnp.max(teacher_logits, axis=1), jnp.max(student_logits, axis=1...  79.3 us
    reduce_scatter x1, waiting for transfers between devices, body(): lax.psum_scatter(lax.dot_general(logit_grad, student_head, (((1,), (1,)),...  71.4 us
    psum x1, blocking collectives, body(): lax.psum((jnp.sum(teacher_expo, axis=1), jnp.sum(student_expo, axis=1)),...  41.2 us
    all_gather x1, waiting for transfers between devices, body(): lax.all_gather(student_hidden, 'dp', axis=0, tiled=True)  30.1 us
    dot_general x1, matrix products, body(): jnp.dot(lax.all_gather(teacher_hidden, 'dp', axis=0, tiled=True), teacher...  25.4 us
    unnamed x3, local copies, waits for them, and re-layouts  19.6 us
    dot_general x1, matrix products, body(): lax.dot_general(student_rows, logit_grad, (((0,), (0,)), ((), ())), prefe...  15.2 us
    dot_general x1, matrix products, body(): jnp.dot(student_rows, student_head, preferred_element_type=jnp.float32)  14.5 us
  transfers between devices with their start and end apart: 4, of which 3 were waited for; matrix products, arithmetic and copies ran while one was open for 13% of the time, Pallas kernels for 0%

commit v1 on v0

--- a/solution.py
+++ b/solution.py
@@ -34,7 +34,7 @@
     teacher_expo = jnp.exp(teacher_logits - teacher_peak[:, None])
     student_expo = jnp.exp(student_logits - student_peak[:, None])
     teacher_total, student_total = lax.psum(
-        (jnp.sum(teacher_expo, axis=1), jnp.sum(student_expo, axis=1)), ("dp", "tensor")
+        lax.psum((jnp.sum(teacher_expo, axis=1), jnp.sum(student_expo, axis=1)), "tensor"), "dp"
     )
     teacher_probs = teacher_expo / teacher_total[:, None]
     student_probs = student_expo / student_total[:, None]

time: 352 us -> 332 us (0.943)
  blocking collectives: 131 us -> 113 us
    psum x1, blocking collectives: 41.2 us -> 10.8 us  [body(): lax.psum((jnp.sum(teacher_expo, axis=1), jnp.sum(student_expo, axis=1)),...]
    psum x0 -> x1, blocking collectives: none -> 12.4 us  [body(): lax.psum(lax.psum((jnp.sum(teacher_expo, axis=1), jnp.sum(student_expo, a...]
  transfers between devices with their start and end apart: 4 -> 4, of which waited for: 3 -> 3; matrix products, arithmetic and copies ran while one was open for 13% -> 14% of each run, Pallas kernels for 0% -> 0%
where the time goes in v1:
time: 332 us
  blocking collectives  113 us (34%)
  waiting for transfers between devices  104 us (31%)
  matrix products  68.4 us (21%)
  local copies, waits for them, and re-layouts  19.6 us (6%)
  between operations  13.8 us (4%)
  other arithmetic  12.9 us (4%)
    pmax x2, blocking collectives, body(): lax.pmax((jnp.max(teacher_logits, axis=1), jnp.max(student_logits, axis=1...  79.3 us
    reduce_scatter x1, waiting for transfers between devices, body(): lax.psum_scatter(lax.dot_general(logit_grad, student_head, (((1,), (1,)),...  69.6 us
    all_gather x1, waiting for transfers between devices, body(): lax.all_gather(student_hidden, 'dp', axis=0, tiled=True)  30.1 us
    dot_general x1, matrix products, body(): jnp.dot(lax.all_gather(teacher_hidden, 'dp', axis=0, tiled=True), teacher...  25.4 us
    unnamed x3, local copies, waits for them, and re-layouts  19.6 us
    dot_general x1, matrix products, body(): lax.dot_general(student_rows, logit_grad, (((0,), (0,)), ((), ())), prefe...  15.2 us
    dot_general x1, matrix products, body(): jnp.dot(student_rows, student_head, preferred_element_type=jnp.float32)  14.5 us
    dot_general x1, matrix products, body(): lax.dot_general(logit_grad, student_head, (((1,), (1,)), ((), ())), prefe...  13.3 us
  transfers between devices with their start and end apart: 4, of which 3 were waited for; matrix products, arithmetic and copies ran while one was open for 14% of the time, Pallas kernels for 0%

profile of v1, /device:TPU:0, one launch (start us, length us, event | category | flops | bytes accessed | tf_op | source)
XLA Modules:
  0.0 331.6 jit_solution(2885545660306120505)
XLA Ops:
  7.2 0.0 all-gather.4.cloned.1.call-start
  7.2 0.7 all-gather.4.cloned.1.call-update
  7.9 0.0 all-gather.6.cloned.1.call-start
  7.9 0.7 all-gather.6.cloned.1.call-update
  8.6 0.0 reduce-scatter.3.cloned.1.call-start
  8.7 10.4 %all-gather = s32[8,1,128]{2,1,0:T(1,128)S(1)} all-gather(s32[1,1,128]{2,1,0:T(1,128)} %bitcast.13), channel_id=1, replica_groups=mesh['dp'=8,'tensor'=4] {'dp'}, dimensions={0}, use_global_device_ids=true | all-gather | bytes 4608 | tf_op jit(solution)/shard_map/all_gather | solution.py:24
  19.1 30.1 %all-gather.4.cloned.1.call-done = bf16[1024,2048]{1,0:T(8,128)(2,1)} async-done(((bf16[128,2048]{1,0:T(8,128)(2,1)}), bf16[1024,2048]{1,0:T(8,128)(2,1)}) %all-gather.4.cloned.1.call-update) | async-done | bytes 4194320 | tf_op jit(solution)/shard_map/all_gather | solution.py:23
  49.2 14.5 %select_reduce_fusion.1 = (f32[1024]{0:T(1024)S(1)}, f32[1024,2048]{1,0:T(8,128)}) fusion(pred[2048]{0:T(1024)(128)(4,1)S(1)} %broadcast_compare_fusion, bf16[1024,2048]{1,0:T(8,128)(2,1)} %all-gather.4.cloned.1.call-done, bf16[2048,2048]{1,0:T(8,128)(2,1)} %param.9), kind=kOutput, calls=%fused_computation.5 | convolution fusion | flops 8594127872 | bytes 20977664 | tf_op jit(solution)/shard_map/dot_general | solution.py:28
  63.7 40.1 %pmax.14 = f32[1024]{0:T(1024)S(1)} all-reduce(f32[1024]{0:T(1024)S(1)} %get-tuple-element.12), channel_id=1, replica_groups=mesh['dp'=8,'tensor'=4] {'dp','tensor'}, use_global_device_ids=true, to_apply=%region_1.2 | all-reduce | flops 1024 | bytes 8192 | tf_op jit(solution)/shard_map/pmax | solution.py:31
  103.8 2.8 all-gather.6.cloned.1.call-done
  106.6 25.4 %fusion = (f32[1024]{0:T(1024)S(1)}, f32[1024]{0:T(1024)S(1)}, f32[1024,2048]{1,0:T(8,128)}) fusion(f32[1024,2048]{1,0:T(8,128)} %get-tuple-element.13, f32[1024]{0:T(1024)S(1)} %pmax.14, pred[2048]{0:T(1024)(128)(4,1)S(1)} %broadcast_compare_fusion, bf16[1024,4096]{1,0:T(8,128)(2,1)} %all-gather.6.cloned.1.call-done, bf16[4096,2048]{1,0:T(8,128)(2,1)} %param.8), kind=kOutput, calls=%fused_computation.6 | convolution fusion | flops 17190354944 | bytes 41957376 | tf_op jit(solution)/shard_map/dot_general | solution.py:16
  132.0 39.3 %pmax.15 = f32[1024]{0:T(1024)S(1)} all-reduce(f32[1024]{0:T(1024)S(1)} %get-tuple-element.7), channel_id=1, replica_groups=mesh['dp'=8,'tensor'=4] {'dp','tensor'}, use_global_device_ids=true, to_apply=%region_6.7 | all-reduce | flops 1024 | bytes 8192 | tf_op jit(solution)/shard_map/pmax | solution.py:31
  171.2 4.4 %fusion.1 = f32[1024]{0:T(1024)S(1)} fusion(f32[1024,2048]{1,0:T(8,128)} %get-tuple-element.14, f32[1024]{0:T(1024)S(1)} %pmax.15, pred[2048]{0:T(1024)(128)(4,1)S(1)} %broadcast_compare_fusion), kind=kLoop, calls=%fused_computation.7 | loop fusion | flops 6290432 | bytes 8398848 | tf_op jit(solution)/shard_map/reduce_sum | solution.py:37
  175.6 10.8 %all-reduce.1 = (f32[1024]{0:T(1024)S(1)}, f32[1024]{0:T(1024)S(1)}) all-reduce(f32[1024]{0:T(1024)S(1)} %fusion.1, f32[1024]{0:T(1024)S(1)} %get-tuple-element.6), channel_id=1, replica_groups=mesh['dp'=8,'tensor'=4] {'tensor'}, use_global_device_ids=true, to_apply=%region_8.9 | all-reduce | flops 2048 | bytes 16384 | tf_op jit(solution)/shard_map/psum | solution.py:37
  186.4 12.4 %all-reduce = (f32[1024]{0:T(1024)S(1)}, f32[1024]{0:T(1024)S(1)}) all-reduce(f32[1024]{0:T(1024)S(1)} %get-tuple-element.10, f32[1024]{0:T(1024)S(1)} %get-tuple-element.11), channel_id=1, replica_groups=mesh['dp'=8,'tensor'=4] {'dp'}, use_global_device_ids=true, to_apply=%region_9.10 | all-reduce | flops 2048 | bytes 16384 | tf_op jit(solution)/shard_map/psum | solution.py:36
  198.8 8.5 %subtract_convert_fusion = bf16[1024,2048]{1,0:T(8,128)(2,1)S(1)} fusion(f32[1024,2048]{1,0:T(8,128)} %get-tuple-element.13, f32[1024,2048]{1,0:T(8,128)} %get-tuple-element.14, s32[2048]{0:T(1024)S(1)} %iota_add_fusion, f32[1024]{0:T(1024)S(1)} %get-tuple-element.8, f32[1024]{0:T(1024)S(1)} %pmax.15, f32[1024]{0:T(1024)S(1)} %get-tuple-element.9, ...), kind=kLoop, calls=%fused_computation.1 | loop fusion | flops 25165824 | bytes 21002240 | tf_op jit(solution)/shard_map/convert_element_type | solution.py:42
  207.3 0.0 copy-start
  207.3 2.0 copy-done
  209.2 13.3 %fusion.2 = f32[1024,2048]{1,0:T(8,128)} fusion(bf16[1024,2048]{1,0:T(8,128)(2,1)S(1)} %subtract_convert_fusion, bf16[2048,2048]{1,0:T(8,128)(2,1)} %param.9), kind=kOutput, calls=%fused_computation.10 | convolution fusion | flops 8589934592 | bytes 20971520 | tf_op jit(solution)/shard_map/dot_general | solution.py:47
  222.5 0.0 reduce-scatter.3.cloned.1.call-update
  222.5 0.0 reduce-scatter.5.cloned.1.call-start
  222.6 69.6 %reduce-scatter.3.cloned.1.call-done = f32[128,2048]{1,0:T(8,128)} async-done(((f32[1024,2048]{1,0:T(8,128)}), f32[128,2048]{1,0:T(8,128)}) %reduce-scatter.3.cloned.1.call-update) | async-done | bytes 1048592 | tf_op jit(solution)/shard_map/reduce_scatter | solution.py:46
  292.2 0.0 reduce-scatter.5.cloned.1.call-update
  292.2 15.2 %convolution_bitcast_fusion = f32[2048,2048]{0,1:T(8,128)} fusion(bf16[1024,2048]{1,0:T(8,128)(2,1)} %copy-done, bf16[1024,2048]{1,0:T(8,128)(2,1)} %all-gather.4.cloned.1.call-done), kind=kOutput, calls=%fused_computation | convolution fusion | flops 8589934592 | bytes 25165824 | tf_op jit(solution)/shard_map/dot_general | solution.py:43
  307.4 17.6 %copy.8 = f32[2048,2048]{1,0:T(8,128)} copy(f32[2048,2048]{0,1:T(8,128)} %convolution_bitcast_fusion) | data formatting | bytes 33554432
  325.0 0.0 reduce-scatter.5.cloned.1.call-done
  (2 shorter events, 0.0 us)
Async XLA Ops:
  7.2 42.0 %all-gather.4.cloned.1.call-start = ((), (), s32[]{:S(2)}) async-start(), calls=%async_computation.2 | async-start | bytes 4718592 | tf_op jit(solution)/shard_map/all_gather | solution.py:23
  7.9 98.7 %all-gather.6.cloned.1.call-start = ((), (), s32[]{:S(2)}) async-start(), calls=%async_computation.3 | async-start | bytes 9437184 | tf_op jit(solution)/shard_map/all_gather | solution.py:17
  8.6 283.5 %reduce-scatter.3.cloned.1.call-start = ((), (), s32[]{:S(2)}) async-start(), calls=%async_computation.4 | async-start | bytes 9437184 | tf_op jit(solution)/shard_map/reduce_scatter | solution.py:46
  207.3 2.0 copy-start
  222.5 102.5 %reduce-scatter.5.cloned.1.call-start = ((), (), s32[]{:S(2)}) async-start(), calls=%async_computation.5 | async-start | bytes 1310720 | tf_op jit(solution)/shard_map/reduce_scatter | solution.py:54
Sparse Core Ops, SparseCore 0:
  9.9 39.2 all-gather.3
  51.1 55.4 all-gather.5
  222.7 69.4 reduce-scatter.2
  294.9 27.2 reduce-scatter.4
